TPU v7x, 32 devices: a whole 2x2x4 slice. The times are simulated.
32 devices in a mesh: gx: 8 (over y, x, core), gy: 4 (over z).
Axes of the slice: x: 2, y: 2, z: 4, core: 2. Of those that a mesh axis runs over, the one named last changes fastest.
Arguments:
- cells: bfloat16 [1024, 256, 128], P('gx', 'gy'), may hold values from -6 to 6
- cotangent: bfloat16 [1024, 256, 128], P('gx', 'gy'), may hold values from -6 to 6
- lift_weight: bfloat16 [128, 512], replicated, may hold values from -0.5 to 0.5
- drop_weight: bfloat16 [512, 128], replicated, may hold values from -0.25 to 0.25
- xmode_weight: bfloat16 [2, 16, 128, 128], P(None, 'gx'), may hold values from -0.375 to 0.375
- ymode_weight: bfloat16 [2, 8, 128, 128], replicated, may hold values from -0.375 to 0.375
- coarse_weight: bfloat16 [128, 128], replicated, may hold values from -0.5 to 0.5
- coarse_mix: bfloat16 [16, 16], replicated, may hold values from -1.5 to 1.5
Outputs:
- cell_grad: bfloat16 [1024, 256, 128], P('gx', 'gy')
- lift_grad: float32 [128, 512], replicated
- drop_grad: float32 [512, 128], replicated
- xmode_grad: float32 [2, 16, 128, 128], P(None, 'gx')
- ymode_grad: float32 [2, 8, 128, 128], replicated
- coarse_weight_grad: float32 [128, 128], replicated
- coarse_mix_grad: float32 [16, 16], replicated
All inputs are finite; a program needn't handle non-finite values.
Results may differ from a plain program's by a relative error of at most 0.006.
Values sent between devices are 32-bit elements; how exact they have to be, the bound alone decides.
A program may use at most 128 MiB of HBM per device.

v0:
```python
import math
import jax
import jax.numpy as jnp
from jax import lax
from jax.sharding import PartitionSpec as P

MODES_X = 16
MODES_Y = 8
POOL = 16
gelu_scale = 0.7978845608028654
gelu_cubic = 0.044715
highest = lax.Precision.HIGHEST


def gelu_value(values):
    tangent = jnp.tanh(gelu_scale * (values + gelu_cubic * values * values * values))
    return 0.5 * values * (1.0 + tangent)


def gelu_slope(values):
    tangent = jnp.tanh(gelu_scale * (values + gelu_cubic * values * values * values))
    return 0.5 * (1.0 + tangent) + 0.5 * values * (1.0 - tangent * tangent) * gelu_scale * (
        1.0 + 3.0 * gelu_cubic * values * values
    )


def mode_basis(mode_count, length, offset, extent):
    frequency = jnp.arange(mode_count, dtype=jnp.int32)
    places = offset + jnp.arange(extent, dtype=jnp.int32)
    phase_index = frequency[:, None] * places[None, :] % length
    angles = phase_index.astype(jnp.float32) * (2.0 * math.pi / length)
    return jnp.concatenate([jnp.cos(angles), -jnp.sin(angles)], axis=0)


def mix_modes(spectrum, weights):

    def product(former, latter):
        return jnp.einsum("mrc,mcd->mrd", former, latter, precision=highest)

    real_out = product(spectrum[0], weights[0]) - product(spectrum[1], weights[1])
    imaginary_out = product(spectrum[0], weights[1]) + product(spectrum[1], weights[0])
    return jnp.stack([real_out, imaginary_out])


def mix_back(spectrum, gradient, weights):

    def contract_cells(former, latter):
        return jnp.einsum("mrc,mrd->mcd", former, latter, precision=highest)

    def contract_channels(former, latter):
        return jnp.einsum("mrd,mcd->mrc", former, latter, precision=highest)

    weight_real = contract_cells(spectrum[0], gradient[0]) + contract_cells(
        spectrum[1], gradient[1]
    )
    weight_imaginary = contract_cells(spectrum[0], gradient[1]) - contract_cells(
        spectrum[1], gradient[0]
    )
    spec_real = contract_channels(gradient[0], weights[0]) + contract_channels(
        gradient[1], weights[1]
    )
    spec_imaginary = contract_channels(gradient[1], weights[0]) - contract_channels(
        gradient[0], weights[1]
    )
    return (jnp.stack([weight_real, weight_imaginary]), jnp.stack([spec_real, spec_imaginary]))


def row_reduce(partial_spec):
    return lax.psum_scatter(partial_spec, "gx", scatter_dimension=1, tiled=True)


def row_return(owned_spec):
    return lax.all_gather(owned_spec, "gx", axis=1, tiled=True)


def column_reduce(partial_spec):
    return lax.psum_scatter(partial_spec, "gy", scatter_dimension=2, tiled=True)


def column_return(owned_spec):
    return lax.all_gather(owned_spec, "gy", axis=2, tiled=True)


def coarse_columns(coarse_block):
    return lax.all_gather(coarse_block, "gy", axis=1, tiled=True)


def upsample(coarse_field, row_count, column_count, channels):
    spread = jnp.broadcast_to(
        coarse_field[:, None, :, None, :],
        (row_count // POOL, POOL, column_count // POOL, POOL, channels),
    )
    return spread.reshape(row_count, column_count, channels)


def on_device(
    cells,
    cotangent,
    lift_weight,
    drop_weight,
    xmode_weight,
    ymode_weight,
    coarse_weight,
    coarse_mix,
):
    row_count, column_count, channels = cells.shape
    row_total = row_count * lax.axis_size("gx")
    column_total = column_count * lax.axis_size("gy")
    coarse_rows = row_count // POOL
    coarse_width = column_count // POOL
    row_basis = mode_basis(MODES_X, row_total, lax.axis_index("gx") * row_count, row_count)
    column_basis = mode_basis(
        MODES_Y, column_total, lax.axis_index("gy") * column_count, column_count
    )
    row_weight = xmode_weight.astype(jnp.float32)
    column_weight = ymode_weight.astype(jnp.float32)
    coarse_float = coarse_weight.astype(jnp.float32)
    mixing_float = coarse_mix.astype(jnp.float32)
    flat_cells = cells.reshape(row_count, column_count * channels)
    row_partial = jnp.dot(
        row_basis.astype(jnp.bfloat16), flat_cells, preferred_element_type=jnp.float32
    ) * (1.0 / math.sqrt(row_total))
    row_owned = row_reduce(row_partial.reshape(2, MODES_X, column_count, channels))
    row_mixed = row_return(mix_modes(row_owned, row_weight))
    row_field = jnp.dot(
        row_basis.T, row_mixed.reshape(2 * MODES_X, column_count * channels), precision=highest
    ) * (1.0 / math.sqrt(MODES_X))
    column_partial = jnp.einsum(
        "ry,xyc->rxc", column_basis.astype(jnp.bfloat16), cells, preferred_element_type=jnp.float32
    ) * (1.0 / math.sqrt(column_total))
    column_owned = column_reduce(column_partial.reshape(2, MODES_Y, row_count, channels))
    column_mixed = column_return(mix_modes(column_owned, column_weight))
    column_field = jnp.einsum(
        "ry,rxc->xyc",
        column_basis,
        column_mixed.reshape(2 * MODES_Y, row_count, channels),
        precision=highest,
    ) * (1.0 / math.sqrt(MODES_Y))
    pooled_own = cells.astype(jnp.float32).reshape(
        coarse_rows, POOL, coarse_width, POOL, channels
    ).sum(axis=(1, 3)) * (1.0 / POOL)
    pooled = coarse_columns(pooled_own)
    coarse_pre = jnp.einsum("ijc,cd->ijd", pooled, coarse_float, precision=highest)
    coarse_act = gelu_value(coarse_pre)
    column_offset = lax.axis_index("gy") * coarse_width
    mixing_rows = lax.dynamic_slice_in_dim(mixing_float, column_offset, coarse_width, 0)
    coarse_own = jnp.einsum("jk,ikc->ijc", mixing_rows, coarse_act, precision=highest)
    summed = (
        row_field.reshape(row_count, column_count, channels)
        + column_field
        + upsample(coarse_own, row_count, column_count, channels)
    )
    ffn_input = summed.reshape(row_count * column_count, channels).astype(jnp.bfloat16)
    hidden_before = jnp.dot(ffn_input, lift_weight, preferred_element_type=jnp.float32)
    hidden_after = gelu_value(hidden_before).astype(jnp.bfloat16)
    cotangent_rows = cotangent.reshape(row_count * column_count, channels)
    drop_partial = jnp.einsum(
        "nf,nc->fc", hidden_after, cotangent_rows, preferred_element_type=jnp.float32
    )
    after_grad = jnp.einsum(
        "nc,fc->nf", cotangent_rows, drop_weight, preferred_element_type=jnp.float32
    )
    before_grad = (after_grad * gelu_slope(hidden_before)).astype(jnp.bfloat16)
    lift_partial = jnp.einsum(
        "nc,nf->cf", ffn_input, before_grad, preferred_element_type=jnp.float32
    )
    summed_grad = jnp.einsum(
        "nf,cf->nc", before_grad, lift_weight, preferred_element_type=jnp.float32
    )
    summed_cells = summed_grad.reshape(row_count, column_count, channels)
    row_back_partial = jnp.dot(
        row_basis, summed_grad.reshape(row_count, column_count * channels), precision=highest
    ) * (1.0 / math.sqrt(MODES_X))
    row_back = row_reduce(row_back_partial.reshape(2, MODES_X, column_count, channels))
    row_weight_partial, row_spec_grad = mix_back(row_owned, row_back, row_weight)
    row_spec_full = row_return(row_spec_grad)
    row_cell_grad = jnp.dot(
        row_basis.T, row_spec_full.reshape(2 * MODES_X, column_count * channels), precision=highest
    ) * (1.0 / math.sqrt(row_total))
    column_back_partial = jnp.einsum(
        "ry,xyc->rxc", column_basis, summed_cells, precision=highest
    ) * (1.0 / math.sqrt(MODES_Y))
    column_back = column_reduce(column_back_partial.reshape(2, MODES_Y, row_count, channels))
    column_weight_partial, column_spec_grad = mix_back(column_owned, column_back, column_weight)
    column_spec_full = column_return(column_spec_grad)
    column_cell_grad = jnp.einsum(
        "ry,rxc->xyc",
        column_basis,
        column_spec_full.reshape(2 * MODES_Y, row_count, channels),
        precision=highest,
    ) * (1.0 / math.sqrt(column_total))
    coarse_grad_own = summed_cells.reshape(coarse_rows, POOL, coarse_width, POOL, channels).sum(
        axis=(1, 3)
    )
    coarse_grad = coarse_columns(coarse_grad_own)
    coarse_act_grad = jnp.einsum("jk,ijc->ikc", mixing_float, coarse_grad, precision=highest)
    mixing_partial = jnp.einsum("ijc,ikc->jk", coarse_grad, coarse_act, precision=highest)
    coarse_pre_grad = coarse_act_grad * gelu_slope(coarse_pre)
    coarse_weight_partial = jnp.einsum("ijc,ijd->cd", pooled, coarse_pre_grad, precision=highest)
    pre_grad_own = lax.dynamic_slice_in_dim(coarse_pre_grad, column_offset, coarse_width, 1)
    pooled_grad = jnp.einsum("ijd,cd->ijc", pre_grad_own, coarse_float, precision=highest) * (
        1.0 / POOL
    )
    cell_grad = (
        cotangent.astype(jnp.float32)
        + row_cell_grad.reshape(row_count, column_count, channels)
        + column_cell_grad
        + upsample(pooled_grad, row_count, column_count, channels)
    ).astype(jnp.bfloat16)
    xmode_grad = lax.psum(row_weight_partial, "gy")
    lift_grad, drop_grad, ymode_grad = lax.psum(
        (lift_partial, drop_partial, column_weight_partial), ("gx", "gy")
    )
    coarse_weight_grad, coarse_mix_grad = lax.psum((coarse_weight_partial, mixing_partial), "gx")
    return (
        cell_grad,
        lift_grad,
        drop_grad,
        xmode_grad,
        ymode_grad,
        coarse_weight_grad,
        coarse_mix_grad,
    )


def solution(mesh):
    in_specs = (
        P("gx", "gy", None),
        P("gx", "gy", None),
        P(),
        P(),
        P(None, "gx", None, None),
        P(),
        P(),
        P(),
    )
    out_specs = (P("gx", "gy", None), P(), P(), P(None, "gx", None, None), P(), P(), P())
    return jax.shard_map(
        on_device, mesh=mesh, in_specs=in_specs, out_specs=out_specs, check_vma=False
    )
```

profile of v0, /device:TPU:0, one launch (start us, length us, event | category | flops | bytes accessed | tf_op | source)
XLA Modules:
  0.0 478.8 jit_solution(4133987111560620458)
XLA Ops:
  8.2 3.1 fusion.17
  11.3 1.2 copy.53
  13.0 1.3 copy.33
  15.6 56.4 %all-reduce.11.cloned.1.call-done = f32[2,16,64,128]{3,2,1,0:T(8,128)} async-done(((f32[2,16,64,128]{3,2,1,0:T(8,128)}), f32[2,16,64,128]{3,2,1,0:T(8,128)}) %all-reduce.11.cloned.1.call-update) | async-done | bytes 1048592
  76.9 1.2 fusion.44
  78.1 1.2 fusion.27
  79.4 1.2 fusion.52
  80.6 1.2 fusion.28
  83.0 13.4 %all_gather.20 = f32[8,16,128]{2,0,1:T(8,128)S(1)} all-gather(f32[8,4,128]{2,0,1:T(8,128)S(1)} %copy_multiply_fusion), channel_id=1, replica_groups=mesh['gx'=8,'gy'=4] {'gy'}, dimensions={1}, use_global_device_ids=true | all-gather | bytes 81920 | tf_op jit(solution)/shard_map/all_gather | solution.py:85
  96.8 2.8 all-gather.5.cloned.1.call-done
  99.6 4.8 %fusion.13 = f32[16,8,64,128]{3,1,2,0:T(8,128)S(1)} fusion(f32[4,8,64,128]{3,2,1,0:T(8,128)} %bitcast.239, f32[16,128]{1,0:T(8,128)S(1)} %get-tuple-element.15, f32[16,128]{1,0:T(8,128)S(1)} %get-tuple-element.14), kind=kOutput, calls=%fused_computation.23 | convolution fusion | flops 403705856 | bytes 5259264 | tf_op jit(solution)/shard_map/dot_general | solution.py:125
  104.4 2.7 copy.55
  107.1 22.7 %all-gather.7.cloned.1.call-done = f32[2,8,128,128]{3,2,1,0:T(8,128)} async-done(((f32[2,8,32,128]{3,2,1,0:T(8,128)}), f32[2,8,128,128]{3,2,1,0:T(8,128)}) %all-gather.7.cloned.1.call-update) | async-done | bytes 1048592 | tf_op jit(solution)/shard_map/all_gather | solution.py:81
  130.2 1.7 copy-done.6
  132.0 5.5 %fusion.12 = bf16[128,64,128]{2,1,0:T(8,128)(2,1)S(1)} fusion(f32[128,64,128]{2,1,0:T(8,128)S(1)} %bitcast.232, f32[16,8,64,128]{3,2,1,0:T(8,128)S(1)} %copy-done.6, f32[16,128,128]{2,1,0:T(8,128)} %bitcast.240, f32[8,64]{1,0:T(8,128)S(1)} %get-tuple-element.13, f32[8,64]{1,0:T(8,128)S(1)} %get-tuple-element.12), kind=kOutput, calls=%fused_computation.21 | convolution fusion | flops 205521920 | bytes 11538432 | tf_op jit(solution)/shard_map/ry,rxc->xyc/dot_general | solution.py:133
  137.5 2.3 fusion.155
  139.8 12.1 %fusion.6 = bf16[8192,512]{1,0:T(8,128)(2,1)S(1)} fusion(f32[8192,512]{1,0:T(8,128)S(1)} %fusion.155, bf16[8192,128]{1,0:T(8,128)(2,1)S(1)} %bitcast.236, bf16[512,128]{1,0:T(8,128)(2,1)S(1)} %copy-done.15), kind=kOutput, calls=%fused_computation.8 | convolution fusion | flops 1153433600 | bytes 27394048 | tf_op jit(solution)/shard_map/nc,fc->nf/dot_general | solution.py:160
  151.9 3.3 copy-done.2
  155.2 4.3 fusion.156
  159.5 5.0 %reshape.90 = f32[128,8192]{1,0:T(8,128)} reshape(f32[8192,128]{1,0:T(8,128)} %fusion.156) | data formatting | bytes 8388608 | tf_op jit(solution)/shard_map/reshape | solution.py:172
  164.5 2.6 reduce_sum.19
  167.1 13.1 %all_gather.23 = f32[8,16,128]{2,0,1:T(8,128)S(1)} all-gather(f32[8,4,128]{2,0,1:T(8,128)S(1)} %copy.39), channel_id=1, replica_groups=mesh['gx'=8,'gy'=4] {'gy'}, dimensions={1}, use_global_device_ids=true | all-gather | bytes 81920 | tf_op jit(solution)/shard_map/all_gather | solution.py:85
  181.4 4.0 fusion.20
  185.4 1.2 copy.56
  186.6 3.8 fusion.21
  190.4 1.3 copy.37
  191.8 51.4 %all-reduce.15.cloned.1.call-done = (f32[2,16,64,128]{3,2,1,0:T(8,128)}, f32[128,128]{1,0:T(8,128)}) async-done(((f32[2,16,64,128]{3,2,1,0:T(8,128)}, f32[128,128]{1,0:T(8,128)}), (f32[2,16,64,128]{3,2,1,0:T(8,128)}, f32[128,128]{1,0:T(8,128)})) %all-reduce.15.cloned.1.call-update) | async-done | bytes 1114128
  248.3 1.4 fusion.47
  249.7 1.4 fusion.25
  251.1 1.4 fusion.49
  252.5 1.4 fusion.26
  254.8 10.9 %fusion.7 = f32[512,128]{1,0:T(8,128)} fusion(bf16[8192,128]{1,0:T(8,128)(2,1)} %bitcast.235, f32[8192,512]{1,0:T(8,128)} %copy-done.3), kind=kOutput, calls=%fused_computation.14 | convolution fusion | flops 1111490560 | bytes 19136512 | tf_op jit(solution)/shard_map/nf,nc->fc/dot_general | solution.py:157
  265.9 5.5 %fusion.157 = f32[128,512]{1,0:T(8,128)} fusion(bf16[8192,128]{1,0:T(8,128)(2,1)S(1)} %bitcast.228, bf16[8192,512]{1,0:T(8,128)(2,1)} %copy-done.2), kind=kOutput, calls=%fused_computation.215 | convolution fusion | flops 1073741824 | bytes 10747904 | tf_op jit(solution)/shard_map/nc,nf->cf/dot_general | solution.py:164
  271.3 1.3 fusion.86
  272.6 1.3 fusion.87
  273.9 1.3 fusion.29
  275.2 1.3 fusion.30
  282.6 13.7 %psum.47 = f32[16,16]{1,0:T(8,128)} all-reduce(f32[16,16]{1,0:T(8,128)S(1)} %convolution_bitcast_fusion.3), channel_id=1, replica_groups=mesh['gx'=8,'gy'=4] {'gx'}, use_global_device_ids=true, to_apply=%region_11.12 | all-reduce | flops 256 | bytes 2048 | tf_op jit(solution)/shard_map/psum | solution.py:214
  296.3 4.8 %fusion.14 = f32[16,8,64,128]{3,1,2,0:T(8,128)S(1)} fusion(f32[4,8,64,128]{3,2,1,0:T(8,128)} %bitcast.237, f32[16,128]{1,0:T(8,128)S(1)} %get-tuple-element.15, f32[16,128]{1,0:T(8,128)S(1)} %get-tuple-element.14), kind=kOutput, calls=%fused_computation.24 | convolution fusion | flops 403705856 | bytes 5259264 | tf_op jit(solution)/shard_map/dot_general | solution.py:177
  301.1 2.7 copy.58
  305.0 1.7 copy-done.5
  306.7 7.0 %fusion.10 = bf16[128,64,128]{2,1,0:T(8,128)(2,1)} fusion(f32[128,64,128]{2,1,0:T(8,128)S(1)} %bitcast.231, f32[16,8,64,128]{3,2,1,0:T(8,128)S(1)} %copy-done.5, bf16[128,64,128]{2,1,0:T(8,128)(2,1)S(1)} %copy-done.12, f32[16,128,128]{2,1,0:T(8,128)} %bitcast.238, f32[8,64]{1,0:T(8,128)S(1)} %get-tuple-element.13, f32[8,64]{1,0:T(8,128)S(1)} %get-tuple-element.12), kind=kOutput, calls=%fused_computation.18 | convolution fusion | flops 207619072 | bytes 13635584 | tf_op jit(solution)/shard_map/ry,rxc->xyc/dot_general | solution.py:186
  313.7 10.4 %all-reduce.9.cloned.1.call-done = f32[2,2,128,128]{3,2,1,0:T(8,128)} async-done(((f32[2,2,128,128]{3,2,1,0:T(8,128)}), f32[2,2,128,128]{3,2,1,0:T(8,128)}) %all-reduce.9.cloned.1.call-update) | async-done | bytes 262160 | tf_op jit(solution)/shard_map/psum | solution.py:210
  324.1 138.9 %all-reduce.13.cloned.1.call-done = (f32[128,512]{1,0:T(8,128)}, f32[512,128]{1,0:T(8,128)}, f32[2,8,128,128]{3,2,1,0:T(8,128)}) async-done(((f32[128,512]{1,0:T(8,128)}, f32[512,128]{1,0:T(8,128)}, f32[2,8,128,128]{3,2,1,0:T(8,128)}), (f32[128,512]{1,0:T(8,128)}, f32[512,128]{1,0:T(8,128)}, f32[2,8,128,128]{3,2,1,0:T(8,128)})) %all-reduce.13.cloned.1.call-update) | async-done | bytes 1572880 | tf_op jit(solution)/shard_map/psum | solution.py:211
  463.0 1.7 copy.95
  464.7 1.7 copy.96
  466.4 1.7 copy.97
  468.0 2.3 copy.98
  (95 shorter events, 23.3 us)
Async XLA Ops:
  8.0 129.4 %copy-start = (bf16[128,512]{1,0:T(8,128)(2,1)S(1)}, bf16[128,512]{1,0:T(8,128)(2,1)}, u32[]{:S(2)}) copy-start(bf16[128,512]{1,0:T(8,128)(2,1)} %param.10) | copy-start | bytes 393220
  8.0 4.6 copy-start.4
  8.0 64.0 %all-reduce.11.cloned.1.call-start = ((), (), s32[]{:S(2)}) async-start(), calls=%async_computation.9 | async-start | bytes 2097152
  12.4 1.9 copy-start.17
  12.4 59.6 %copy-start.10 = (bf16[2,2,128,128]{3,2,1,0:T(8,128)(2,1)S(1)}, bf16[2,2,128,128]{3,2,1,0:T(8,128)(2,1)}, u32[]{:S(2)}) copy-start(bf16[2,2,128,128]{3,2,1,0:T(8,128)(2,1)} %param.12) | copy-start | bytes 393220
  12.4 64.5 %copy-start.7 = (bf16[2,8,128,128]{3,2,1,0:T(8,128)(2,1)S(1)}, bf16[2,8,128,128]{3,2,1,0:T(8,128)(2,1)}, u32[]{:S(2)}) copy-start(bf16[2,8,128,128]{3,2,1,0:T(8,128)(2,1)} %param.13) | copy-start | bytes 1572868
  12.4 64.5 %reduce-scatter.9.cloned.1.call-start = ((), (), s32[]{:S(2)}) async-start(), calls=%async_computation.3 | async-start | bytes 1310720 | tf_op jit(solution)/shard_map/reduce_scatter | solution.py:77
  14.3 82.2 %copy-start.13 = (bf16[128,128]{1,0:T(8,128)(2,1)S(1)}, bf16[128,128]{1,0:T(8,128)(2,1)}, u32[]{:S(2)}) copy-start(bf16[128,128]{1,0:T(8,128)(2,1)} %param.14) | copy-start | bytes 98308
  14.3 82.3 %copy-start.16 = (bf16[16,16]{1,0:T(8,128)(2,1)S(1)}, bf16[16,16]{1,0:T(8,128)(2,1)}, u32[]{:S(2)}) copy-start(bf16[16,16]{1,0:T(8,128)(2,1)} %param.15) | copy-start | bytes 1540
  14.3 85.3 %all-gather.5.cloned.1.call-start = ((), (), s32[]{:S(2)}) async-start(), calls=%async_computation.2 | async-start | bytes 1179648 | tf_op jit(solution)/shard_map/all_gather | solution.py:73
  76.8 52.9 %all-gather.7.cloned.1.call-start = ((), (), s32[]{:S(2)}) async-start(), calls=%async_computation.4 | async-start | bytes 1310720 | tf_op jit(solution)/shard_map/all_gather | solution.py:81
  82.6 160.6 %all-reduce.15.cloned.1.call-start = ((), (), s32[]{:S(2)}) async-start(), calls=%async_computation.11 | async-start | bytes 2228224
  129.8 2.2 copy-start.6
  137.5 2.4 copy-start.11
  137.5 2.4 copy-start.15
  139.8 12.1 %copy-start.3 = (f32[8192,512]{1,0:T(8,128)}, f32[8192,512]{1,0:T(8,128)S(1)}, u32[]{:S(2)}) copy-start(f32[8192,512]{1,0:T(8,128)S(1)} %fusion.155) | copy-start | bytes 50331652
  151.9 3.3 copy-start.2
  186.5 61.7 %reduce-scatter.11.cloned.1.call-start = ((), (), s32[]{:S(2)}) async-start(), calls=%async_computation.6 | async-start | bytes 1310720 | tf_op jit(solution)/shard_map/reduce_scatter | solution.py:77
  191.8 104.5 %all-gather.9.cloned.1.call-start = ((), (), s32[]{:S(2)}) async-start(), calls=%async_computation.5 | async-start | bytes 1179648 | tf_op jit(solution)/shard_map/all_gather | solution.py:73
  248.2 56.3 %all-gather.11.cloned.1.call-start = ((), (), s32[]{:S(2)}) async-start(), calls=%async_computation.7 | async-start | bytes 1310720 | tf_op jit(solution)/shard_map/all_gather | solution.py:81
  254.7 69.4 %all-reduce.9.cloned.1.call-start = ((), (), s32[]{:S(2)}) async-start(), calls=%async_computation.8 | async-start | bytes 524288 | tf_op jit(solution)/shard_map/psum | solution.py:210
  265.8 11.4 %copy-start.8 = (f32[2,8,32,128]{3,2,1,0:T(8,128)S(1)}, f32[2,8,32,128]{3,2,1,0:T(8,128)}, u32[]{:S(2)}) copy-start(f32[2,8,32,128]{3,2,1,0:T(8,128)} %reduce-scatter.9.cloned.1.call-done) | copy-start | bytes 786436
  265.9 11.4 %copy-start.9 = (f32[2,8,32,128]{3,2,1,0:T(8,128)S(1)}, f32[2,8,32,128]{3,2,1,0:T(8,128)}, u32[]{:S(2)}) copy-start(f32[2,8,32,128]{3,2,1,0:T(8,128)} %reduce-scatter.11.cloned.1.call-done) | copy-start | bytes 786436
  277.2 185.8 %all-reduce.13.cloned.1.call-start = ((), (), s32[]{:S(2)}) async-start(), calls=%async_computation.10 | async-start | bytes 3145728 | tf_op jit(solution)/shard_map/psum | solution.py:211
  301.1 3.9 copy-start.12
  304.5 2.2 copy-start.5
  306.7 163.6 %copy-start.14 = (f32[128,128]{1,0:T(8,128)S(1)}, f32[128,128]{1,0:T(8,128)}, u32[]{:S(2)}) copy-start(f32[128,128]{1,0:T(8,128)} %get-tuple-element.21) | copy-start | bytes 196612
  306.7 164.2 %copy-start.1 = (bf16[128,512]{1,0:T(8,128)(2,1)S(1)}, bf16[128,512]{1,0:T(8,128)(2,1)}, u32[]{:S(2)}) copy-start(bf16[128,512]{1,0:T(8,128)(2,1)} %param.10) | copy-start | bytes 393220
Sparse Core Ops, SparseCore 0:
  12.6 59.4 all-reduce.10
  76.9 22.6 all-gather.4
  101.8 27.9 all-gather.6
  186.7 56.4 all-reduce.14
  248.3 22.6 all-gather.8
  273.0 31.4 all-gather.10
Sparse Core Ops, SparseCore 1:
  15.8 29.9 reduce-scatter.8
  191.8 26.6 reduce-scatter.10
  277.3 46.8 all-reduce.8
  330.4 132.5 all-reduce.12
where the time goes:
time: 484 us; the launch traced here: 479 us
  waiting for transfers between devices  283 us (58%)
  matrix products  98.3 us (20%)
  blocking collectives  40.2 us (8%)
  local copies, waits for them, and re-layouts  31.6 us (7%)
  between operations  17.1 us (4%)
  other arithmetic  7.65 us (2%)
    psum x1, waiting for transfers between devices, on_device(): lax.psum((lift_partial, drop_partial, column_weight_partial), ('gx', 'gy'))  139 us
    unnamed x12, waiting for transfers between devices  108 us
    all_gather x2, blocking collectives, coarse_columns(): return lax.all_gather(coarse_block, 'gy', axis=1, tiled=True)  26.5 us
    all_gather x2, waiting for transfers between devices, column_return(): return lax.all_gather(owned_spec, 'gy', axis=2, tiled=True)  23.4 us
    unnamed x46, local copies, waits for them, and re-layouts  23 us
    psum x1, blocking collectives, on_device(): lax.psum((coarse_weight_partial, mixing_partial), 'gx')  13.7 us
    dot_general x1, matrix products, on_device(): jnp.einsum('nc,fc->nf', cotangent_rows, drop_weight, preferred_element_ty...  12.1 us
    dot_general x1, matrix products, on_device(): jnp.einsum('nf,nc->fc', hidden_after, cotangent_rows, preferred_element_t...  10.9 us
  transfers between devices with their start and end apart: 10, of which 7 were waited for; matrix products, arithmetic and copies ran while one was open for 17% of the time, Pallas kernels for 0%

commit v1 on v0

--- a/solution.py
+++ b/solution.py
@@ -209,7 +209,8 @@
     ).astype(jnp.bfloat16)
     xmode_grad = lax.psum(row_weight_partial, "gy")
     lift_grad, drop_grad, ymode_grad = lax.psum(
-        (lift_partial, drop_partial, column_weight_partial), ("gx", "gy")
+        lax.psum((lift_partial, drop_partial, column_weight_partial), axis_name="gy"),
+        axis_name="gx",
     )
     coarse_weight_grad, coarse_mix_grad = lax.psum((coarse_weight_partial, mixing_partial), "gx")
     return (

time: 484 us -> 422 us (0.87)
  waiting for transfers between devices: 283 us -> 227 us
  matrix products: 98.3 us -> 91.1 us
    psum x1, waiting for transfers between devices: 139 us -> 40.8 us  [on_device(): lax.psum((lift_partial, drop_partial, column_weight_partial), axis_name='...]
    all_gather x2, waiting for transfers between devices: 23.4 us -> 46.2 us  [column_return(): return lax.all_gather(owned_spec, 'gy', axis=2, tiled=True)]
    unnamed x12, waiting for transfers between devices: 108 us -> 126 us
    reduce_scatter x2, waiting for transfers between devices: 0.05 us -> 10.5 us  [column_reduce(): return lax.psum_scatter(partial_spec, 'gy', scatter_dimension=2, tiled=True)]
    psum x1, waiting for transfers between devices: 10.4 us -> 0.01 us  [on_device(): xmode_grad = lax.psum(row_weight_partial, 'gy')]
    unnamed x46 -> x54, local copies, waits for them, and re-layouts: 23 us -> 23.6 us
  transfers between devices with their start and end apart: 10 -> 10, of which waited for: 7 -> 8; matrix products, arithmetic and copies ran while one was open for 17% -> 17% of each run, Pallas kernels for 0% -> 0%
where the time goes in v1:
time: 422 us; the launch traced here: 417 us
  waiting for transfers between devices  227 us (54%)
  matrix products  91.1 us (22%)
  blocking collectives  40.8 us (10%)
  local copies, waits for them, and re-layouts  32.2 us (8%)
  between operations  17.3 us (4%)
  other arithmetic  7.63 us (2%)
    unnamed x12, waiting for transfers between devices  126 us
    all_gather x2, waiting for transfers between devices, column_return(): return lax.all_gather(owned_spec, 'gy', axis=2, tiled=True)  46.2 us
    psum x1, waiting for transfers between devices, on_device(): lax.psum((lift_partial, drop_partial, column_weight_partial), axis_name='...  40.8 us
    all_gather x2, blocking collectives, coarse_columns(): return lax.all_gather(coarse_block, 'gy', axis=1, tiled=True)  27.5 us
    unnamed x54, local copies, waits for them, and re-layouts  23.6 us
    psum x1, blocking collectives, on_device(): lax.psum((coarse_weight_partial, mixing_partial), 'gx')  13.3 us
    dot_general x8, matrix products, contract_cells(): return jnp.einsum('mrc,mrd->mcd', former, latter, precision=highest)  12.7 us
    dot_general x1, matrix products, on_device(): jnp.einsum('nc,fc->nf', cotangent_rows, drop_weight, preferred_element_ty...  11.7 us
  transfers between devices with their start and end apart: 10, of which 8 were waited for; matrix products, arithmetic and copies ran while one was open for 17% of the time, Pallas kernels for 0%

profile of v1, /device:TPU:0, one launch (start us, length us, event | category | flops | bytes accessed | tf_op | source)
XLA Modules:
  0.0 416.8 jit_solution(14394584376802943580)
XLA Ops:
  8.2 3.1 fusion.17
  11.3 1.2 copy.53
  13.0 1.3 copy.33
  15.6 56.4 %all-reduce.11.cloned.1.call-done = f32[2,16,64,128]{3,2,1,0:T(8,128)} async-done(((f32[2,16,64,128]{3,2,1,0:T(8,128)}), f32[2,16,64,128]{3,2,1,0:T(8,128)}) %all-reduce.11.cloned.1.call-update) | async-done | bytes 1048592
  76.9 1.2 fusion.44
  78.1 1.2 fusion.27
  79.4 1.2 fusion.52
  80.6 1.2 fusion.28
  83.0 13.6 %all_gather.20 = f32[8,16,128]{2,0,1:T(8,128)S(1)} all-gather(f32[8,4,128]{2,0,1:T(8,128)S(1)} %copy_multiply_fusion), channel_id=1, replica_groups=mesh['gx'=8,'gy'=4] {'gy'}, dimensions={1}, use_global_device_ids=true | all-gather | bytes 81920 | tf_op jit(solution)/shard_map/all_gather | solution.py:85
  97.0 2.6 all-gather.5.cloned.1.call-done
  99.6 4.8 %fusion.13 = f32[16,8,64,128]{3,1,2,0:T(8,128)S(1)} fusion(f32[4,8,64,128]{3,2,1,0:T(8,128)} %bitcast.239, f32[16,128]{1,0:T(8,128)S(1)} %get-tuple-element.18, f32[16,128]{1,0:T(8,128)S(1)} %get-tuple-element.17), kind=kOutput, calls=%fused_computation.23 | convolution fusion | flops 403705856 | bytes 5259264 | tf_op jit(solution)/shard_map/dot_general | solution.py:125
  104.4 2.7 copy.55
  107.1 22.6 %all-gather.7.cloned.1.call-done = f32[2,8,128,128]{3,2,1,0:T(8,128)} async-done(((f32[2,8,32,128]{3,2,1,0:T(8,128)}), f32[2,8,128,128]{3,2,1,0:T(8,128)}) %all-gather.7.cloned.1.call-update) | async-done | bytes 1048592 | tf_op jit(solution)/shard_map/all_gather | solution.py:81
  130.2 1.7 copy-done.8
  132.0 5.5 %fusion.12 = bf16[128,64,128]{2,1,0:T(8,128)(2,1)S(1)} fusion(f32[128,64,128]{2,1,0:T(8,128)S(1)} %bitcast.232, f32[16,8,64,128]{3,2,1,0:T(8,128)S(1)} %copy-done.8, f32[16,128,128]{2,1,0:T(8,128)} %bitcast.240, f32[8,64]{1,0:T(8,128)S(1)} %get-tuple-element.16, f32[8,64]{1,0:T(8,128)S(1)} %get-tuple-element.15), kind=kOutput, calls=%fused_computation.21 | convolution fusion | flops 205521920 | bytes 11538432 | tf_op jit(solution)/shard_map/ry,rxc->xyc/dot_general | solution.py:133
  137.5 2.3 fusion.155
  139.8 11.7 %fusion.6 = bf16[8192,512]{1,0:T(8,128)(2,1)S(1)} fusion(f32[8192,512]{1,0:T(8,128)S(1)} %fusion.155, bf16[8192,128]{1,0:T(8,128)(2,1)S(1)} %bitcast.236, bf16[512,128]{1,0:T(8,128)(2,1)S(1)} %copy-done.19), kind=kOutput, calls=%fused_computation.8 | convolution fusion | flops 1153433600 | bytes 27394048 | tf_op jit(solution)/shard_map/nc,fc->nf/dot_general | solution.py:160
  151.6 2.3 fusion.156
  154.8 2.0 copy-done.3
  156.8 2.1 fusion.21
  158.9 1.3 copy.37
  160.3 5.5 %fusion.157 = f32[128,512]{1,0:T(8,128)} fusion(bf16[8192,128]{1,0:T(8,128)(2,1)S(1)} %bitcast.228, bf16[8192,512]{1,0:T(8,128)(2,1)} %copy-done.2), kind=kOutput, calls=%fused_computation.215 | convolution fusion | flops 1073741824 | bytes 10747904 | tf_op jit(solution)/shard_map/nc,nf->cf/dot_general | solution.py:164
  165.8 2.9 copy-done.5
  168.7 7.7 %fusion.7 = f32[512,128]{1,0:T(8,128)} fusion(bf16[8192,128]{1,0:T(8,128)(2,1)} %bitcast.235, f32[8192,512]{1,0:T(8,128)S(1)} %copy-done.5), kind=kOutput, calls=%fused_computation.14 | convolution fusion | flops 1111490560 | bytes 19136512 | tf_op jit(solution)/shard_map/nf,nc->fc/dot_general | solution.py:157
  176.4 10.5 %reduce-scatter.11.cloned.1.call-done = f32[2,8,32,128]{3,2,1,0:T(8,128)} async-done(((f32[2,8,128,128]{3,2,1,0:T(8,128)}), f32[2,8,32,128]{3,2,1,0:T(8,128)}) %reduce-scatter.11.cloned.1.call-update) | async-done | bytes 262160 | tf_op jit(solution)/shard_map/reduce_scatter | solution.py:77
  186.9 1.9 fusion.62
  188.8 1.9 fusion.63
  190.7 1.9 fusion.23
  192.6 1.9 fusion.24
  195.9 4.9 %reshape.90 = f32[128,8192]{1,0:T(8,128)} reshape(f32[8192,128]{1,0:T(8,128)} %copy-done.3) | data formatting | bytes 8388608 | tf_op jit(solution)/shard_map/reshape | solution.py:172
  200.8 2.6 reduce_sum.19
  203.4 4.0 fusion.20
  207.4 1.2 copy.56
  208.6 13.9 %all_gather.23 = f32[8,16,128]{2,0,1:T(8,128)S(1)} all-gather(f32[8,4,128]{2,0,1:T(8,128)S(1)} %copy.39), channel_id=1, replica_groups=mesh['gx'=8,'gy'=4] {'gy'}, dimensions={1}, use_global_device_ids=true | all-gather | bytes 81920 | tf_op jit(solution)/shard_map/all_gather | solution.py:85
  223.6 40.8 %all-reduce.15.cloned.1.call-done = (f32[128,512]{1,0:T(8,128)}, f32[512,128]{1,0:T(8,128)}, f32[2,8,128,128]{3,2,1,0:T(8,128)}) async-done(((f32[128,512]{1,0:T(8,128)}, f32[512,128]{1,0:T(8,128)}, f32[2,8,128,128]{3,2,1,0:T(8,128)}), (f32[128,512]{1,0:T(8,128)}, f32[512,128]{1,0:T(8,128)}, f32[2,8,128,128]{3,2,1,0:T(8,128)})) %all-reduce.15.cloned.1.call-update) | async-done | bytes 1572880 | tf_op jit(solution)/shard_map/psum | solution.py:212
  264.5 69.5 %all-reduce.13.cloned.1.call-done = (f32[2,16,64,128]{3,2,1,0:T(8,128)}, f32[128,512]{1,0:T(8,128)}, f32[512,128]{1,0:T(8,128)}, f32[2,8,128,128]{3,2,1,0:T(8,128)}, f32[128,128]{1,0:T(8,128)}) async-done(((f32[2,16,64,128]{3,2,1,0:T(8,128)}, f32[128,512]{1,0:T(8,128)}, f32[512,128]{1,0:T(8,128)}, f32[2,8,128,128]{3,2,1,0:T(8,128)}, f32[128,128]{1,0:T(8,128)}), (f32[2,16,64,128]{3,2,1,0:T(8,128)}, ...) | async-done | bytes 2686992
  342.3 13.3 %psum.71 = f32[16,16]{1,0:T(8,128)} all-reduce(f32[16,16]{1,0:T(8,128)S(1)} %convolution_bitcast_fusion.3), channel_id=1, replica_groups=mesh['gx'=8,'gy'=4] {'gx'}, use_global_device_ids=true, to_apply=%region_14.15 | all-reduce | flops 256 | bytes 2048 | tf_op jit(solution)/shard_map/psum | solution.py:215
  355.6 1.3 fusion.86
  356.9 1.3 fusion.87
  358.1 1.3 fusion.29
  359.4 1.3 fusion.30
  362.4 4.8 %fusion.14 = f32[16,8,64,128]{3,1,2,0:T(8,128)S(1)} fusion(f32[4,8,64,128]{3,2,1,0:T(8,128)} %bitcast.237, f32[16,128]{1,0:T(8,128)S(1)} %get-tuple-element.18, f32[16,128]{1,0:T(8,128)S(1)} %get-tuple-element.17), kind=kOutput, calls=%fused_computation.24 | convolution fusion | flops 403705856 | bytes 5259264 | tf_op jit(solution)/shard_map/dot_general | solution.py:177
  367.3 2.7 copy.58
  370.0 23.6 %all-gather.11.cloned.1.call-done = f32[2,8,128,128]{3,2,1,0:T(8,128)} async-done(((f32[2,8,32,128]{3,2,1,0:T(8,128)}), f32[2,8,128,128]{3,2,1,0:T(8,128)}) %all-gather.11.cloned.1.call-update) | async-done | bytes 1048592 | tf_op jit(solution)/shard_map/all_gather | solution.py:81
  394.0 1.7 copy-done.7
  395.8 7.0 %fusion.10 = bf16[128,64,128]{2,1,0:T(8,128)(2,1)} fusion(f32[128,64,128]{2,1,0:T(8,128)S(1)} %bitcast.231, f32[16,8,64,128]{3,2,1,0:T(8,128)S(1)} %copy-done.7, bf16[128,64,128]{2,1,0:T(8,128)(2,1)S(1)} %copy-done.14, f32[16,128,128]{2,1,0:T(8,128)} %bitcast.238, f32[8,64]{1,0:T(8,128)S(1)} %get-tuple-element.16, f32[8,64]{1,0:T(8,128)S(1)} %get-tuple-element.15), kind=kOutput, calls=%fused_computation.18 | convolution fusion | flops 207619072 | bytes 13635584 | tf_op jit(solution)/shard_map/ry,rxc->xyc/dot_general | solution.py:186
  404.2 1.7 copy.100
  405.9 2.3 copy.101
  (103 shorter events, 24.2 us)
Async XLA Ops:
  8.0 129.4 %copy-start = (bf16[128,512]{1,0:T(8,128)(2,1)S(1)}, bf16[128,512]{1,0:T(8,128)(2,1)}, u32[]{:S(2)}) copy-start(bf16[128,512]{1,0:T(8,128)(2,1)} %param.10) | copy-start | bytes 393220
  8.0 4.6 %copy-start.6 = (bf16[128,64,128]{2,1,0:T(8,128)(2,1)S(1)}, bf16[128,64,128]{2,1,0:T(8,128)(2,1)}, u32[]{:S(2)}) copy-start(bf16[128,64,128]{2,1,0:T(8,128)(2,1)} %param.8) | copy-start | bytes 6291460
  8.0 64.0 %all-reduce.11.cloned.1.call-start = ((), (), s32[]{:S(2)}) async-start(), calls=%async_computation.9 | async-start | bytes 2097152
  12.4 1.9 copy-start.21
  12.4 59.6 %copy-start.12 = (bf16[2,2,128,128]{3,2,1,0:T(8,128)(2,1)S(1)}, bf16[2,2,128,128]{3,2,1,0:T(8,128)(2,1)}, u32[]{:S(2)}) copy-start(bf16[2,2,128,128]{3,2,1,0:T(8,128)(2,1)} %param.12) | copy-start | bytes 393220
  12.4 64.5 %copy-start.9 = (bf16[2,8,128,128]{3,2,1,0:T(8,128)(2,1)S(1)}, bf16[2,8,128,128]{3,2,1,0:T(8,128)(2,1)}, u32[]{:S(2)}) copy-start(bf16[2,8,128,128]{3,2,1,0:T(8,128)(2,1)} %param.13) | copy-start | bytes 1572868
  12.4 64.5 %reduce-scatter.9.cloned.1.call-start = ((), (), s32[]{:S(2)}) async-start(), calls=%async_computation.3 | async-start | bytes 1310720 | tf_op jit(solution)/shard_map/reduce_scatter | solution.py:77
  14.3 82.3 %copy-start.17 = (bf16[128,128]{1,0:T(8,128)(2,1)S(1)}, bf16[128,128]{1,0:T(8,128)(2,1)}, u32[]{:S(2)}) copy-start(bf16[128,128]{1,0:T(8,128)(2,1)} %param.14) | copy-start | bytes 98308
  14.3 82.5 %copy-start.20 = (bf16[16,16]{1,0:T(8,128)(2,1)S(1)}, bf16[16,16]{1,0:T(8,128)(2,1)}, u32[]{:S(2)}) copy-start(bf16[16,16]{1,0:T(8,128)(2,1)} %param.15) | copy-start | bytes 1540
  14.3 85.3 %all-gather.5.cloned.1.call-start = ((), (), s32[]{:S(2)}) async-start(), calls=%async_computation.2 | async-start | bytes 1179648 | tf_op jit(solution)/shard_map/all_gather | solution.py:73
  76.8 52.9 %all-gather.7.cloned.1.call-start = ((), (), s32[]{:S(2)}) async-start(), calls=%async_computation.4 | async-start | bytes 1310720 | tf_op jit(solution)/shard_map/all_gather | solution.py:81
  82.6 104.3 %reduce-scatter.11.cloned.1.call-start = ((), (), s32[]{:S(2)}) async-start(), calls=%async_computation.6 | async-start | bytes 1310720 | tf_op jit(solution)/shard_map/reduce_scatter | solution.py:77
  129.8 2.2 copy-start.8
  137.5 2.4 copy-start.13
  137.5 2.4 copy-start.19
  139.8 11.7 %copy-start.4 = (f32[8192,512]{1,0:T(8,128)}, f32[8192,512]{1,0:T(8,128)S(1)}, u32[]{:S(2)}) copy-start(f32[8192,512]{1,0:T(8,128)S(1)} %fusion.155) | copy-start | bytes 50331652
  151.6 3.3 copy-start.2
  154.8 2.0 copy-start.3
  160.2 104.2 %all-reduce.15.cloned.1.call-start = ((), (), s32[]{:S(2)}) async-start(), calls=%async_computation.11 | async-start | bytes 3145728 | tf_op jit(solution)/shard_map/psum | solution.py:212
  160.3 8.4 %copy-start.5 = (f32[8192,512]{1,0:T(8,128)S(1)}, f32[8192,512]{1,0:T(8,128)}, u32[]{:S(2)}) copy-start(f32[8192,512]{1,0:T(8,128)} %copy-done.4) | copy-start | bytes 50331652
  168.7 18.2 %copy-start.10 = (f32[2,8,32,128]{3,2,1,0:T(8,128)S(1)}, f32[2,8,32,128]{3,2,1,0:T(8,128)}, u32[]{:S(2)}) copy-start(f32[2,8,32,128]{3,2,1,0:T(8,128)} %reduce-scatter.9.cloned.1.call-done) | copy-start | bytes 786436
  195.6 138.3 %all-reduce.13.cloned.1.call-start = ((), (), s32[]{:S(2)}) async-start(), calls=%async_computation.10 | async-start | bytes 5373952
  207.4 131.6 %copy-start.11 = (f32[2,8,32,128]{3,2,1,0:T(8,128)S(1)}, f32[2,8,32,128]{3,2,1,0:T(8,128)}, u32[]{:S(2)}) copy-start(f32[2,8,32,128]{3,2,1,0:T(8,128)} %reduce-scatter.11.cloned.1.call-done) | copy-start | bytes 786436
  264.4 98.0 %all-gather.9.cloned.1.call-start = ((), (), s32[]{:S(2)}) async-start(), calls=%async_computation.5 | async-start | bytes 1179648 | tf_op jit(solution)/shard_map/all_gather | solution.py:73
  339.0 54.6 %all-gather.11.cloned.1.call-start = ((), (), s32[]{:S(2)}) async-start(), calls=%async_computation.7 | async-start | bytes 1310720 | tf_op jit(solution)/shard_map/all_gather | solution.py:81
  341.9 61.0 %all-reduce.9.cloned.1.call-start = ((), (), s32[]{:S(2)}) async-start(), calls=%async_computation.8 | async-start | bytes 524288 | tf_op jit(solution)/shard_map/psum | solution.py:210
  367.3 26.8 %copy-start.14 = (bf16[128,64,128]{2,1,0:T(8,128)(2,1)S(1)}, bf16[128,64,128]{2,1,0:T(8,128)(2,1)}, u32[]{:S(2)}) copy-start(bf16[128,64,128]{2,1,0:T(8,128)(2,1)} %param.9) | copy-start | bytes 6291460
  393.6 2.2 copy-start.7
  395.8 7.1 %copy-start.16 = (f32[128,512]{1,0:T(8,128)S(1)}, f32[128,512]{1,0:T(8,128)}, u32[]{:S(2)}) copy-start(f32[128,512]{1,0:T(8,128)} %get-tuple-element.20) | copy-start | bytes 786436
  395.8 7.8 %copy-start.15 = (f32[512,128]{1,0:T(8,128)S(1)}, f32[512,128]{1,0:T(8,128)}, u32[]{:S(2)}) copy-start(f32[512,128]{1,0:T(8,128)} %get-tuple-element.21) | copy-start | bytes 786436
  395.8 12.4 %copy-start.18 = (f32[128,128]{1,0:T(8,128)S(1)}, f32[128,128]{1,0:T(8,128)}, u32[]{:S(2)}) copy-start(f32[128,128]{1,0:T(8,128)} %get-tuple-element.24) | copy-start | bytes 196612
  395.8 13.1 %copy-start.1 = (bf16[128,512]{1,0:T(8,128)(2,1)S(1)}, bf16[128,512]{1,0:T(8,128)(2,1)}, u32[]{:S(2)}) copy-start(bf16[128,512]{1,0:T(8,128)(2,1)} %param.10) | copy-start | bytes 393220
Sparse Core Ops, SparseCore 0:
  12.6 59.4 all-reduce.10
  76.9 22.6 all-gather.4
  101.8 27.9 all-gather.6
  195.7 68.6 all-reduce.14
  268.6 65.2 all-reduce.12
  339.1 23.3 all-gather.8
  364.6 28.9 all-gather.10
Sparse Core Ops, SparseCore 1:
  15.8 29.9 reduce-scatter.8
  160.3 26.5 reduce-scatter.10
  361.5 40.1 all-reduce.8
